TPU v7x, 128 devices: a whole 4x4x4 slice. The times are simulated.
128 devices in a mesh: section: 2 (over z_hi), expert: 8 (over y, z_lo), dp: 8 (over x, core).
Axes of the slice: x: 4, y: 4, z: 4 (z_hi: 2, z_lo: 2; z = z_hi * 2 + z_lo), core: 2. Of those that a mesh axis runs over, the one named last changes fastest.
Arguments:
- inputs: bfloat16 [2, 512, 3072], P(None, ('expert', 'dp')), may hold values from -6 to 6
- cotangent: bfloat16 [2, 512, 3072], P(None, ('expert', 'dp')), may hold values from -6 to 6
- norm_gain: bfloat16 [2, 3072], P('section'), may hold values from 0.5 to 1.5
- router: bfloat16 [2, 3072, 8], P('section'), may hold values from -0.109375 to 0.109375
- w_gate: bfloat16 [2, 8, 3072, 8192], P('section', 'expert', None, 'dp'), may hold values from -0.109375 to 0.109375
- w_up: bfloat16 [2, 8, 3072, 8192], P('section', 'expert', None, 'dp'), may hold values from -0.109375 to 0.109375
- w_down: bfloat16 [2, 8, 8192, 3072], P('section', 'expert', 'dp'), may hold values from -0.0625 to 0.0625
- routes: int32 [2, 2, 512, 2], P('section', None, ('expert', 'dp')), may hold values from 0 to 7, as said below
Outputs:
- acts: bfloat16 [2, 2, 512, 3072], P('section', None, ('expert', 'dp'))
- grads: bfloat16 [2, 2, 512, 3072], P('section', None, ('expert', 'dp'))
- router_grad: float32 [2, 3072, 8], P('section')
Inputs may be any that keep to these rules, and one draw needn't show every extreme that they name: `routes`: the two experts of a token differ. For each layer and micro-batch, the 8 tokens of one device name no expert more than 3 times, and one expert, the same on all devices for that layer and micro-batch, exactly 3 times.
All inputs are finite; a program needn't handle non-finite values.
Results may differ from a plain program's by a relative error of at most 0.017.
Values may be sent and summed in bfloat16 or wider, within the bound.
A program may use at most 128 MiB of HBM per device.

v0:
```python
import jax
import jax.numpy as jnp
from jax import lax
from jax.sharding import PartitionSpec as P

EPSILON = 1e-05


def passed_along(block, axis, distance):
    devices = range(lax.axis_size(axis))
    route = [(i - distance, i) for i in devices if i - distance in devices]
    return lax.ppermute(block, axis, route)


def norm_rows(layer_in, gain_row):
    values = layer_in.astype(jnp.float32)
    inv_rms = lax.rsqrt(jnp.mean(values * values, axis=-1, keepdims=True) + EPSILON)
    return (values, inv_rms, (values * inv_rms * gain_row).astype(jnp.bfloat16))


def gate_probs(hidden, router_w, picks):
    logits = jnp.dot(hidden, router_w, preferred_element_type=jnp.float32)
    chosen = jnp.take_along_axis(logits, picks, axis=1)
    logit_gap = chosen[:, 0] - chosen[:, 1]
    return jnp.stack([jax.nn.sigmoid(logit_gap), jax.nn.sigmoid(-logit_gap)], axis=1)


def slot_table(picks, experts, capacity):
    flat_pick = picks.reshape(-1)
    onehot = (flat_pick[:, None] == jnp.arange(experts, dtype=jnp.int32)[None, :]).astype(jnp.int32)
    earlier = jnp.cumsum(onehot, axis=0) - onehot
    slot_pos = jnp.sum(earlier * onehot, axis=1)
    target = flat_pick * capacity + slot_pos
    return target[:, None] == jnp.arange(experts * capacity, dtype=jnp.int32)[None, :]


def deliver(outgoing, experts, capacity):
    model_width = outgoing.shape[1]
    grouped = outgoing.reshape(experts, capacity, model_width)
    tiled = jnp.repeat(grouped, lax.axis_size("dp"), axis=0)
    arrived = lax.all_to_all(tiled, ("expert", "dp"), split_axis=0, concat_axis=0, tiled=True)
    return arrived.reshape(-1, model_width)


def collect(partial_out, experts, capacity):
    model_width = partial_out.shape[1]
    replicas = lax.axis_size("dp")
    returned = lax.all_to_all(
        partial_out.reshape(experts * replicas, capacity, model_width),
        ("expert", "dp"),
        split_axis=0,
        concat_axis=0,
        tiled=True,
    )
    summed = jnp.sum(
        returned.reshape(experts, replicas, capacity, model_width).astype(jnp.float32), axis=1
    )
    return summed.reshape(experts * capacity, model_width)


def send_rows(placing, row_values):
    grouped = lax.dot_general(
        placing.astype(jnp.bfloat16),
        row_values,
        (((0,), (0,)), ((), ())),
        preferred_element_type=jnp.float32,
    )
    return grouped.astype(jnp.bfloat16)


def forward_layer(layer_in, picks, gain_row, router_w, gate_w, up_w, down_w, experts, capacity):
    values, inv_rms, hidden = norm_rows(layer_in, gain_row)
    gate_prob = gate_probs(hidden, router_w, picks)
    placing = slot_table(picks, experts, capacity)
    arrived = deliver(
        send_rows(placing, jnp.repeat(hidden, picks.shape[1], axis=0)), experts, capacity
    )
    gate_pre = jnp.dot(arrived, gate_w, preferred_element_type=jnp.float32)
    up_pre = jnp.dot(arrived, up_w, preferred_element_type=jnp.float32)
    active = (gate_pre * jax.nn.sigmoid(gate_pre) * up_pre).astype(jnp.bfloat16)
    partial_out = jnp.dot(active, down_w, preferred_element_type=jnp.float32).astype(jnp.bfloat16)
    summed = collect(partial_out, experts, capacity)
    picked = jnp.dot(placing.astype(jnp.float32), summed, precision=lax.Precision.HIGHEST)
    picked = picked.reshape(layer_in.shape[0], picks.shape[1], -1)
    layer_out = (values + jnp.sum(gate_prob[:, :, None] * picked, axis=1)).astype(jnp.bfloat16)
    return (layer_out, picked, gate_pre, up_pre)


def backward_layer(
    layer_in,
    upstream,
    picks,
    gain_row,
    router_w,
    gate_w,
    up_w,
    down_w,
    picked,
    gate_pre,
    up_pre,
    experts,
    capacity,
):
    values, inv_rms, hidden = norm_rows(layer_in, gain_row)
    gate_prob = gate_probs(hidden, router_w, picks)
    placing = slot_table(picks, experts, capacity)
    grad_out = upstream.astype(jnp.float32)
    d_prob = jnp.sum(grad_out[:, None, :] * picked, axis=2)
    d_gap = gate_prob[:, 0] * gate_prob[:, 1] * (d_prob[:, 0] - d_prob[:, 1])
    d_chosen = jnp.stack([d_gap, -d_gap], axis=1)
    expert_hot = (picks[:, :, None] == jnp.arange(experts, dtype=jnp.int32)[None, None, :]).astype(
        jnp.float32
    )
    d_logits = jnp.sum(d_chosen[:, :, None] * expert_hot, axis=1)
    scaled = (gate_prob[:, :, None] * grad_out[:, None, :]).astype(jnp.bfloat16)
    scaled = scaled.reshape(-1, grad_out.shape[1])
    arrived = deliver(send_rows(placing, scaled), experts, capacity)
    contract_last = (((1,), (1,)), ((), ()))
    d_active = lax.dot_general(arrived, down_w, contract_last, preferred_element_type=jnp.float32)
    gate_sig = jax.nn.sigmoid(gate_pre)
    d_gate = (d_active * up_pre * gate_sig * (1.0 + gate_pre * (1.0 - gate_sig))).astype(
        jnp.bfloat16
    )
    d_up = (d_active * gate_pre * gate_sig).astype(jnp.bfloat16)
    d_rows = lax.dot_general(d_gate, gate_w, contract_last, preferred_element_type=jnp.float32)
    d_rows = d_rows + lax.dot_general(d_up, up_w, contract_last, preferred_element_type=jnp.float32)
    summed = collect(d_rows.astype(jnp.bfloat16), experts, capacity)
    returned = jnp.dot(placing.astype(jnp.float32), summed, precision=lax.Precision.HIGHEST)
    returned = returned.reshape(layer_in.shape[0], picks.shape[1], -1)
    d_hidden = jnp.sum(returned, axis=1) + jnp.dot(
        d_logits, router_w.astype(jnp.float32).T, precision=lax.Precision.HIGHEST
    )
    router_term = jnp.dot(hidden.astype(jnp.float32).T, d_logits, precision=lax.Precision.HIGHEST)
    weighted = gain_row * d_hidden
    cubed = inv_rms * inv_rms * inv_rms
    d_in = (
        grad_out
        + inv_rms * weighted
        - values * cubed * jnp.mean(values * weighted, axis=-1, keepdims=True)
    )
    return (d_in.astype(jnp.bfloat16), router_term)


def fetch_micro(stored, which_mb):
    return lax.dynamic_index_in_dim(stored, which_mb, 0, keepdims=False)


def store_micro(stored, fresh, which_mb, in_range):
    previous = lax.dynamic_index_in_dim(stored, which_mb, 0, keepdims=False)
    return lax.dynamic_update_index_in_dim(
        stored, jnp.where(in_range, fresh, previous), which_mb, 0
    )


def per_device(inputs, cotangent, norm_gain, router, w_gate, w_up, w_down, routes):
    section_count = lax.axis_size("section")
    section_id = lax.axis_index("section")
    micro_count, tok_rows, model_width = inputs.shape
    experts = router.shape[2]
    top_k = routes.shape[3]
    capacity = 3 * top_k * tok_rows // (2 * experts)
    gate_w = w_gate[0, 0]
    up_w = w_up[0, 0]
    down_w = w_down[0, 0]
    gain_row = norm_gain[0].astype(jnp.float32)
    router_w = router[0]
    picks_all = routes[0]
    expert_rows = experts * lax.axis_size("dp") * capacity
    hidden_units = gate_w.shape[1]
    tick_count = micro_count + section_count - 1
    carried = jnp.zeros((tok_rows, model_width), jnp.bfloat16)
    outputs_all = jnp.zeros((micro_count, tok_rows, model_width), jnp.bfloat16)
    stash_in = jnp.zeros((micro_count, tok_rows, model_width), jnp.bfloat16)
    stash_pick = jnp.zeros((micro_count, tok_rows, top_k, model_width), jnp.float32)
    stash_gate = jnp.zeros((micro_count, expert_rows, hidden_units), jnp.float32)
    stash_up = jnp.zeros((micro_count, expert_rows, hidden_units), jnp.float32)
    for moment in range(tick_count):
        position = moment - section_id
        in_range = (position >= 0) & (position < micro_count)
        which_mb = jnp.clip(position, 0, micro_count - 1)
        layer_in = jnp.where(section_id == 0, fetch_micro(inputs, which_mb), carried)
        picks = fetch_micro(picks_all, which_mb)
        layer_out, picked, gate_pre, up_pre = forward_layer(
            layer_in, picks, gain_row, router_w, gate_w, up_w, down_w, experts, capacity
        )
        outputs_all = store_micro(outputs_all, layer_out, which_mb, in_range)
        stash_in = store_micro(stash_in, layer_in, which_mb, in_range)
        stash_pick = store_micro(stash_pick, picked, which_mb, in_range)
        stash_gate = store_micro(stash_gate, gate_pre, which_mb, in_range)
        stash_up = store_micro(stash_up, up_pre, which_mb, in_range)
        if moment + 1 < tick_count:
            carried = passed_along(layer_out, "section", 1)
    carried = jnp.zeros((tok_rows, model_width), jnp.bfloat16)
    grads_all = jnp.zeros((micro_count, tok_rows, model_width), jnp.bfloat16)
    router_sum = jnp.zeros((model_width, experts), jnp.float32)
    for moment in range(tick_count):
        position = moment - (section_count - 1 - section_id)
        in_range = (position >= 0) & (position < micro_count)
        which_mb = jnp.clip(position, 0, micro_count - 1)
        upstream = jnp.where(
            section_id == section_count - 1, fetch_micro(cotangent, which_mb), carried
        )
        d_in, router_term = backward_layer(
            fetch_micro(stash_in, which_mb),
            upstream,
            fetch_micro(picks_all, which_mb),
            gain_row,
            router_w,
            gate_w,
            up_w,
            down_w,
            fetch_micro(stash_pick, which_mb),
            fetch_micro(stash_gate, which_mb),
            fetch_micro(stash_up, which_mb),
            experts,
            capacity,
        )
        grads_all = store_micro(grads_all, d_in, which_mb, in_range)
        router_sum = router_sum + jnp.where(in_range, router_term, 0.0)
        if moment + 1 < tick_count:
            carried = passed_along(d_in, "section", -1)
    router_total = lax.psum(router_sum, ("expert", "dp"))
    return (outputs_all[None], grads_all[None], router_total[None])


def solution(mesh):
    placed = (
        P(None, ("expert", "dp"), None),
        P(None, ("expert", "dp"), None),
        P("section", None),
        P("section", None, None),
        P("section", "expert", None, "dp"),
        P("section", "expert", None, "dp"),
        P("section", "expert", "dp", None),
        P("section", None, ("expert", "dp"), None),
    )
    return jax.shard_map(
        per_device,
        mesh=mesh,
        in_specs=placed,
        out_specs=(
            P("section", None, ("expert", "dp"), None),
            P("section", None, ("expert", "dp"), None),
            P("section", None, None),
        ),
        check_vma=False,
    )
```

profile of v0, /device:TPU:0, one launch (start us, length us, event | category | flops | bytes accessed | tf_op | source)
XLA Modules:
  0.0 985.6 jit_solution(17254181758903616295)
XLA Ops:
  13.8 9.5 all-to-all-start
  30.7 16.1 %all-to-all-done = bf16[64,3,3072]{2,1,0:T(4,128)(2,1)S(1)} async-done(((bf16[64,3,3072]{2,1,0:T(4,128)(2,1)}), bf16[64,3,3072]{2,1,0:T(4,128)(2,1)S(1)}, u32[]{:S(2)}, u32[]{:S(2)}) %all-to-all-start) | async-done | bytes 1179680 | tf_op jit(solution)/shard_map/all_to_all | solution.py:41
  61.3 5.1 all-to-all-start.1
  71.7 18.2 %all-to-all-done.1 = bf16[64,3,3072]{2,1,0:T(4,128)(2,1)S(1)} async-done(((bf16[64,3,3072]{2,1,0:T(4,128)(2,1)}), bf16[64,3,3072]{2,1,0:T(4,128)(2,1)S(1)}, u32[]{:S(2)}, u32[]{:S(2)}) %all-to-all-start.1) | async-done | bytes 1179680 | tf_op jit(solution)/shard_map/all_to_all | solution.py:48
  92.8 5.4 collective-permute-start
  104.4 5.7 all-to-all-start.2
  113.1 20.3 %all-to-all-done.2 = bf16[64,3,3072]{2,1,0:T(4,128)(2,1)} async-done(((bf16[64,3,3072]{2,1,0:T(4,128)(2,1)}), bf16[64,3,3072]{2,1,0:T(4,128)(2,1)}, u32[]{:S(2)}, u32[]{:S(2)}) %all-to-all-start.2) | async-done | bytes 1179680 | tf_op jit(solution)/shard_map/all_to_all | solution.py:41
  136.4 5.4 bitcast_dynamic-update-slice_fusion.4
  148.0 5.1 all-to-all-start.3
  155.6 20.9 %all-to-all-done.3 = bf16[64,3,3072]{2,1,0:T(4,128)(2,1)S(1)} async-done(((bf16[64,3,3072]{2,1,0:T(4,128)(2,1)}), bf16[64,3,3072]{2,1,0:T(4,128)(2,1)S(1)}, u32[]{:S(2)}, u32[]{:S(2)}) %all-to-all-start.3) | async-done | bytes 1179680 | tf_op jit(solution)/shard_map/all_to_all | solution.py:48
  189.5 6.0 all-to-all-start.4
  197.9 20.9 %all-to-all-done.4 = bf16[64,3,3072]{2,1,0:T(4,128)(2,1)} async-done(((bf16[64,3,3072]{2,1,0:T(4,128)(2,1)}), bf16[64,3,3072]{2,1,0:T(4,128)(2,1)}, u32[]{:S(2)}, u32[]{:S(2)}) %all-to-all-start.4) | async-done | bytes 1179680 | tf_op jit(solution)/shard_map/all_to_all | solution.py:41
  221.8 5.4 bitcast_dynamic-update-slice_fusion.3
  240.3 21.5 %all-to-all-done.5 = bf16[64,3,3072]{2,1,0:T(4,128)(2,1)S(1)} async-done(((bf16[64,3,3072]{2,1,0:T(4,128)(2,1)}), bf16[64,3,3072]{2,1,0:T(4,128)(2,1)S(1)}, u32[]{:S(2)}, u32[]{:S(2)}) %all-to-all-start.5) | async-done | bytes 1179680 | tf_op jit(solution)/shard_map/all_to_all | solution.py:48
  267.0 5.8 all-to-all-start.6
  275.1 21.1 %all-to-all-done.6 = bf16[64,3,3072]{2,1,0:T(4,128)(2,1)} async-done(((bf16[64,3,3072]{2,1,0:T(4,128)(2,1)}), bf16[64,3,3072]{2,1,0:T(4,128)(2,1)}, u32[]{:S(2)}, u32[]{:S(2)}) %all-to-all-start.6) | async-done | bytes 1179680 | tf_op jit(solution)/shard_map/all_to_all | solution.py:41
  299.0 5.1 fusion.4
  312.3 5.0 all-to-all-start.7
  318.1 22.5 %all-to-all-done.7 = bf16[64,3,3072]{2,1,0:T(4,128)(2,1)S(1)} async-done(((bf16[64,3,3072]{2,1,0:T(4,128)(2,1)}), bf16[64,3,3072]{2,1,0:T(4,128)(2,1)S(1)}, u32[]{:S(2)}, u32[]{:S(2)}) %all-to-all-start.7) | async-done | bytes 1179680 | tf_op jit(solution)/shard_map/all_to_all | solution.py:48
  344.5 5.2 collective-permute-done.2
  352.6 5.8 all-to-all-start.8
  359.3 22.4 %all-to-all-done.8 = bf16[64,3,3072]{2,1,0:T(4,128)(2,1)} async-done(((bf16[64,3,3072]{2,1,0:T(4,128)(2,1)}), bf16[64,3,3072]{2,1,0:T(4,128)(2,1)}, u32[]{:S(2)}, u32[]{:S(2)}) %all-to-all-start.8) | async-done | bytes 1179680 | tf_op jit(solution)/shard_map/all_to_all | solution.py:41
  385.7 5.5 fusion.2
  399.3 4.9 all-to-all-start.9
  405.5 22.2 %all-to-all-done.9 = bf16[64,3,3072]{2,1,0:T(4,128)(2,1)S(1)} async-done(((bf16[64,3,3072]{2,1,0:T(4,128)(2,1)}), bf16[64,3,3072]{2,1,0:T(4,128)(2,1)S(1)}, u32[]{:S(2)}, u32[]{:S(2)}) %all-to-all-start.9) | async-done | bytes 1179680 | tf_op jit(solution)/shard_map/all_to_all | solution.py:48
  430.6 6.2 collective-permute-done.3
  439.6 5.9 all-to-all-start.10
  446.0 22.9 %all-to-all-done.10 = bf16[64,3,3072]{2,1,0:T(4,128)(2,1)} async-done(((bf16[64,3,3072]{2,1,0:T(4,128)(2,1)}), bf16[64,3,3072]{2,1,0:T(4,128)(2,1)}, u32[]{:S(2)}, u32[]{:S(2)}) %all-to-all-start.10) | async-done | bytes 1179680 | tf_op jit(solution)/shard_map/all_to_all | solution.py:41
  472.8 5.5 fusion
  486.4 5.1 all-to-all-start.11
  493.0 21.9 %all-to-all-done.11 = bf16[64,3,3072]{2,1,0:T(4,128)(2,1)S(1)} async-done(((bf16[64,3,3072]{2,1,0:T(4,128)(2,1)}), bf16[64,3,3072]{2,1,0:T(4,128)(2,1)S(1)}, u32[]{:S(2)}, u32[]{:S(2)}) %all-to-all-start.11) | async-done | bytes 1179680 | tf_op jit(solution)/shard_map/all_to_all | solution.py:48
  516.5 460.3 %all-reduce.2.cloned.1.call-done = f32[1,3072,8]{1,2,0:T(8,128)} async-done(((f32[1,3072,8]{1,2,0:T(8,128)}), f32[1,3072,8]{1,2,0:T(8,128)}) %all-reduce.2.cloned.1.call-update) | async-done | bytes 98320 | tf_op jit(solution)/shard_map/psum | solution.py:222
  (484 shorter events, 150.3 us)
Async XLA Ops:
  13.8 33.0 %all-to-all-start = ((bf16[64,3,3072]{2,1,0:T(4,128)(2,1)}), bf16[64,3,3072]{2,1,0:T(4,128)(2,1)S(1)}, u32[]{:S(2)}, u32[]{:S(2)}) async-start(bf16[64,3,3072]{2,1,0:T(4,128)(2,1)} %bitcast.7), calls=%async_computation | async-start | bytes 3145728 | tf_op jit(solution)/shard_map/all_to_all | solution.py:41
  30.7 36.4 %copy-start.24 = (f32[8,3072]{1,0:T(8,128)}, f32[8,3072]{1,0:T(8,128)S(1)}, u32[]{:S(2)}) copy-start(f32[8,3072]{1,0:T(8,128)S(1)} %bitcast_convert_fusion) | copy-start | bytes 294916
  57.0 41.2 %copy-start.1 = (f32[2,192,1024]{2,1,0:T(8,128)}, f32[2,192,1024]{2,1,0:T(8,128)S(1)}, u32[]{:S(2)}) copy-start(f32[2,192,1024]{2,1,0:T(8,128)S(1)} %get-tuple-element.57) | copy-start | bytes 4718596
  61.3 28.5 %all-to-all-start.1 = ((bf16[64,3,3072]{2,1,0:T(4,128)(2,1)}), bf16[64,3,3072]{2,1,0:T(4,128)(2,1)S(1)}, u32[]{:S(2)}, u32[]{:S(2)}) async-start(bf16[64,3,3072]{2,1,0:T(4,128)(2,1)} %reshape.574), calls=%async_computation.1 | async-start | bytes 3145728 | tf_op jit(solution)/shard_map/all_to_all | solution.py:48
  69.6 22.8 %copy-start.54 = (s32[8,2]{0,1:T(2,128)S(1)}, s32[8,2]{0,1:T(2,128)}, u32[]{:S(2)}) copy-start(s32[8,2]{0,1:T(2,128)} %multiply_add_fusion.5) | copy-start | bytes 196
  92.8 8.0 collective-permute-start
  104.4 29.0 %all-to-all-start.2 = ((bf16[64,3,3072]{2,1,0:T(4,128)(2,1)}), bf16[64,3,3072]{2,1,0:T(4,128)(2,1)}, u32[]{:S(2)}, u32[]{:S(2)}) async-start(bf16[64,3,3072]{2,1,0:T(4,128)(2,1)} %bitcast.17), calls=%async_computation.2 | async-start | bytes 3145728 | tf_op jit(solution)/shard_map/all_to_all | solution.py:41
  148.0 28.5 %all-to-all-start.3 = ((bf16[64,3,3072]{2,1,0:T(4,128)(2,1)}), bf16[64,3,3072]{2,1,0:T(4,128)(2,1)S(1)}, u32[]{:S(2)}, u32[]{:S(2)}) async-start(bf16[64,3,3072]{2,1,0:T(4,128)(2,1)} %reshape.580), calls=%async_computation.3 | async-start | bytes 3145728 | tf_op jit(solution)/shard_map/all_to_all | solution.py:48
  155.6 23.6 %copy-start.53 = (s32[8,2]{0,1:T(2,128)S(1)}, s32[8,2]{0,1:T(2,128)}, u32[]{:S(2)}) copy-start(s32[8,2]{0,1:T(2,128)} %multiply_add_fusion.4) | copy-start | bytes 196
  155.6 29.7 %copy-start.4 = (f32[2,192,1024]{2,1,0:T(8,128)S(1)}, f32[2,192,1024]{2,1,0:T(8,128)}, u32[]{:S(2)}) copy-start(f32[2,192,1024]{2,1,0:T(8,128)} %copy-done.3) | copy-start | bytes 4718596
  180.3 6.7 collective-permute-start.1
  189.5 29.4 %all-to-all-start.4 = ((bf16[64,3,3072]{2,1,0:T(4,128)(2,1)}), bf16[64,3,3072]{2,1,0:T(4,128)(2,1)}, u32[]{:S(2)}, u32[]{:S(2)}) async-start(bf16[64,3,3072]{2,1,0:T(4,128)(2,1)} %bitcast.26), calls=%async_computation.4 | async-start | bytes 3145728 | tf_op jit(solution)/shard_map/all_to_all | solution.py:41
  233.4 28.4 %all-to-all-start.5 = ((bf16[64,3,3072]{2,1,0:T(4,128)(2,1)}), bf16[64,3,3072]{2,1,0:T(4,128)(2,1)S(1)}, u32[]{:S(2)}, u32[]{:S(2)}) async-start(bf16[64,3,3072]{2,1,0:T(4,128)(2,1)} %reshape.586), calls=%async_computation.5 | async-start | bytes 3145728 | tf_op jit(solution)/shard_map/all_to_all | solution.py:48
  240.3 22.7 %copy-start.18 = (f32[2,8,2,3072]{3,1,2,0:T(8,128)S(1)}, f32[2,8,2,3072]{3,1,2,0:T(8,128)}, u32[]{:S(2)}) copy-start(f32[2,8,2,3072]{3,1,2,0:T(8,128)} %copy-done.17) | copy-start | bytes 1179652
  240.3 22.7 %copy-start.35 = (f32[1,8,2,3072]{3,1,2,0:T(8,128)S(1)}, f32[1,8,2,3072]{3,1,2,0:T(8,128)}, u32[]{:S(2)}) copy-start(f32[1,8,2,3072]{3,1,2,0:T(8,128)} %constant_dynamic-slice_fusion.6) | copy-start | bytes 589828
  267.0 37.1 %slice-start = ((s8[6291456]{0:T(1024)(128)(4,1)}), s8[2097152]{0:T(1024)(128)(4,1)S(1)}, s32[]{:S(2)}) async-start(s8[6291456]{0:T(1024)(128)(4,1)} %bitcast.549), calls=%async_computation.13 | async-start | bytes 4194304
  267.0 29.1 %all-to-all-start.6 = ((bf16[64,3,3072]{2,1,0:T(4,128)(2,1)}), bf16[64,3,3072]{2,1,0:T(4,128)(2,1)}, u32[]{:S(2)}, u32[]{:S(2)}) async-start(bf16[64,3,3072]{2,1,0:T(4,128)(2,1)} %bitcast.569), calls=%async_computation.6 | async-start | bytes 3145728 | tf_op jit(solution)/shard_map/all_to_all | solution.py:41
  312.3 28.4 %all-to-all-start.7 = ((bf16[64,3,3072]{2,1,0:T(4,128)(2,1)}), bf16[64,3,3072]{2,1,0:T(4,128)(2,1)S(1)}, u32[]{:S(2)}, u32[]{:S(2)}) async-start(bf16[64,3,3072]{2,1,0:T(4,128)(2,1)} %reshape.592), calls=%async_computation.7 | async-start | bytes 3145728 | tf_op jit(solution)/shard_map/all_to_all | solution.py:48
  318.1 24.0 %copy-start.39 = (bf16[2,8,3072]{2,1,0:T(8,128)(2,1)S(1)}, bf16[2,8,3072]{2,1,0:T(8,128)(2,1)}, u32[]{:S(2)}) copy-start(bf16[2,8,3072]{2,1,0:T(8,128)(2,1)} %param.11) | copy-start | bytes 294916
  318.1 24.0 %copy-start.59 = (f32[8]{0:T(128)S(1)}, f32[8]{0:T(128)}, u32[]{:S(2)}) copy-start(f32[8]{0:T(128)} %copy-done.58) | copy-start | bytes 100
  318.1 24.0 %copy-start.70 = (f32[8]{0:T(128)S(1)}, f32[8]{0:T(128)}, u32[]{:S(2)}) copy-start(f32[8]{0:T(128)} %get-tuple-element.49) | copy-start | bytes 100
  342.3 7.5 collective-permute-start.2
  352.6 38.6 %slice-start.2 = ((s8[6291456]{0:T(1024)(128)(4,1)}), s8[2097152]{0:T(1024)(128)(4,1)S(1)}, s32[]{:S(2)}) async-start(s8[6291456]{0:T(1024)(128)(4,1)} %bitcast.551), calls=%async_computation.15 | async-start | bytes 4194304
  352.6 29.2 %all-to-all-start.8 = ((bf16[64,3,3072]{2,1,0:T(4,128)(2,1)}), bf16[64,3,3072]{2,1,0:T(4,128)(2,1)}, u32[]{:S(2)}, u32[]{:S(2)}) async-start(bf16[64,3,3072]{2,1,0:T(4,128)(2,1)} %bitcast.567), calls=%async_computation.8 | async-start | bytes 3145728 | tf_op jit(solution)/shard_map/all_to_all | solution.py:41
  399.3 28.4 %all-to-all-start.9 = ((bf16[64,3,3072]{2,1,0:T(4,128)(2,1)}), bf16[64,3,3072]{2,1,0:T(4,128)(2,1)S(1)}, u32[]{:S(2)}, u32[]{:S(2)}) async-start(bf16[64,3,3072]{2,1,0:T(4,128)(2,1)} %reshape.598), calls=%async_computation.9 | async-start | bytes 3145728 | tf_op jit(solution)/shard_map/all_to_all | solution.py:48
  429.3 7.5 collective-permute-start.3
  439.6 38.7 %slice-start.4 = ((s8[6291456]{0:T(1024)(128)(4,1)}), s8[2097152]{0:T(1024)(128)(4,1)S(1)}, s32[]{:S(2)}) async-start(s8[6291456]{0:T(1024)(128)(4,1)} %bitcast.553), calls=%async_computation.17 | async-start | bytes 4194304
  439.6 29.2 %all-to-all-start.10 = ((bf16[64,3,3072]{2,1,0:T(4,128)(2,1)}), bf16[64,3,3072]{2,1,0:T(4,128)(2,1)}, u32[]{:S(2)}, u32[]{:S(2)}) async-start(bf16[64,3,3072]{2,1,0:T(4,128)(2,1)} %bitcast.568), calls=%async_computation.10 | async-start | bytes 3145728 | tf_op jit(solution)/shard_map/all_to_all | solution.py:41
  486.4 28.5 %all-to-all-start.11 = ((bf16[64,3,3072]{2,1,0:T(4,128)(2,1)}), bf16[64,3,3072]{2,1,0:T(4,128)(2,1)S(1)}, u32[]{:S(2)}, u32[]{:S(2)}) async-start(bf16[64,3,3072]{2,1,0:T(4,128)(2,1)} %reshape.604), calls=%async_computation.11 | async-start | bytes 3145728 | tf_op jit(solution)/shard_map/all_to_all | solution.py:48
  491.5 485.3 %all-reduce.2.cloned.1.call-start = ((), (), s32[]{:S(2)}) async-start(), calls=%async_computation.12 | async-start | bytes 196608 | tf_op jit(solution)/shard_map/psum | solution.py:222
  491.6 24.2 %copy-start.43 = (bf16[1,2,8,3072]{3,2,1,0:T(8,128)(2,1)}, bf16[1,2,8,3072]{3,2,1,0:T(8,128)(2,1)S(1)}, u32[]{:S(2)}) copy-start(bf16[1,2,8,3072]{3,2,1,0:T(8,128)(2,1)S(1)} %fusion.176) | copy-start | bytes 294916
  516.5 461.8 %copy-start.42 = (bf16[1,2,8,3072]{3,2,1,0:T(8,128)(2,1)}, bf16[1,2,8,3072]{3,2,1,0:T(8,128)(2,1)S(1)}, u32[]{:S(2)}) copy-start(bf16[1,2,8,3072]{3,2,1,0:T(8,128)(2,1)S(1)} %fusion.188) | copy-start | bytes 294916
  (80 other events, 451.5 us)
Sparse Core Ops, SparseCore 0:
  495.3 481.3 all-reduce.1
where the time goes:
time: 996 us; the launch traced here: 986 us
  waiting for transfers between devices  723 us (73%)
  starting transfers between devices  81.9 us (8%)
  local copies, waits for them, and re-layouts  79.4 us (8%)
  matrix products  65.2 us (7%)
  other arithmetic  19.5 us (2%)
  between operations  16.4 us (2%)
    psum x1, waiting for transfers between devices, per_device(): router_total = lax.psum(router_sum, ('expert', 'dp'))  460 us
    all_to_all x6, waiting for transfers between devices, collect(): lax.all_to_all(partial_out.reshape(experts * replicas, capacity, model_wi...  127 us
    all_to_all x6, waiting for transfers between devices, deliver(): lax.all_to_all(tiled, ('expert', 'dp'), split_axis=0, concat_axis=0, tile...  124 us
    all_to_all x6, starting transfers between devices, deliver(): lax.all_to_all(tiled, ('expert', 'dp'), split_axis=0, concat_axis=0, tile...  38.8 us
    all_to_all x6, starting transfers between devices, collect(): lax.all_to_all(partial_out.reshape(experts * replicas, capacity, model_wi...  30.1 us
  transfers between devices with their start and end apart: 17, of which 16 were waited for; matrix products, arithmetic and copies ran while one was open for 3% of the time, Pallas kernels for 0%

commit v1 on v0

--- a/solution.py
+++ b/solution.py
@@ -219,7 +219,7 @@
         router_sum = router_sum + jnp.where(in_range, router_term, 0.0)
         if moment + 1 < tick_count:
             carried = passed_along(d_in, "section", -1)
-    router_total = lax.psum(router_sum, ("expert", "dp"))
+    router_total = jnp.sum(lax.all_gather(router_sum, axis_name=("expert", "dp")), axis=0)
     return (outputs_all[None], grads_all[None], router_total[None])
 
 

time: 996 us -> 588 us (0.59)
  waiting for transfers between devices: 723 us -> 290 us
  blocking collectives: 0 us -> 32.3 us
    psum x1 -> x0, waiting for transfers between devices: 460 us -> none  [per_device(): router_total = lax.psum(router_sum, ('expert', 'dp'))]
    all_gather x0 -> x1, waiting for transfers between devices: none -> 42.6 us  [per_device(): lax.all_gather(router_sum, axis_name=('expert', 'dp'))]
    all_to_all x0 -> x1, blocking collectives: none -> 32.3 us  [deliver(): lax.all_to_all(tiled, ('expert', 'dp'), split_axis=0, concat_axis=0, tile...]
    all_to_all x6 -> x5, waiting for transfers between devices: 124 us -> 103 us  [deliver(): lax.all_to_all(tiled, ('expert', 'dp'), split_axis=0, concat_axis=0, tile...]
    all_to_all x6 -> x5, starting transfers between devices: 38.8 us -> 33 us  [deliver(): lax.all_to_all(tiled, ('expert', 'dp'), split_axis=0, concat_axis=0, tile...]
  transfers between devices with their start and end apart: 17 -> 16, of which waited for: 16 -> 15; matrix products, arithmetic and copies ran while one was open for 3% -> 8% of each run, Pallas kernels for 0% -> 0%
where the time goes in v1:
time: 588 us; the launch traced here: 577 us
  waiting for transfers between devices  290 us (49%)
  starting transfers between devices  76.5 us (13%)
  local copies, waits for them, and re-layouts  75.5 us (13%)
  matrix products  65.1 us (11%)
  blocking collectives  32.3 us (5%)
  other arithmetic  21.9 us (4%)
  between operations  16.3 us (3%)
    all_to_all x6, waiting for transfers between devices, collect(): lax.all_to_all(partial_out.reshape(experts * replicas, capacity, model_wi...  132 us
    all_to_all x5, waiting for transfers between devices, deliver(): lax.all_to_all(tiled, ('expert', 'dp'), split_axis=0, concat_axis=0, tile...  103 us
    all_gather x1, waiting for transfers between devices, per_device(): lax.all_gather(router_sum, axis_name=('expert', 'dp'))  42.6 us
    all_to_all x5, starting transfers between devices, deliver(): lax.all_to_all(tiled, ('expert', 'dp'), split_axis=0, concat_axis=0, tile...  33 us
    all_to_all x1, blocking collectives, deliver(): lax.all_to_all(tiled, ('expert', 'dp'), split_axis=0, concat_axis=0, tile...  32.3 us
    all_to_all x6, starting transfers between devices, collect(): lax.all_to_all(partial_out.reshape(experts * replicas, capacity, model_wi...  30.3 us
    reshape x6, local copies, waits for them, and re-layouts, deliver(): return arrived.reshape(-1, model_width)  17.6 us
    dot_general x3, matrix products, backward_layer(): lax.dot_general(arrived, down_w, contract_last, preferred_element_type=jn...  16.2 us
  transfers between devices with their start and end apart: 16, of which 15 were waited for; matrix products, arithmetic and copies ran while one was open for 8% of the time, Pallas kernels for 0%

profile of v1, /device:TPU:0, one launch (start us, length us, event | category | flops | bytes accessed | tf_op | source)
XLA Modules:
  0.0 577.1 jit_solution(6347327815988128766)
XLA Ops:
  13.8 9.5 %all-to-all-start = ((bf16[64,3,3072]{2,1,0:T(4,128)(2,1)}), bf16[64,3,3072]{2,1,0:T(4,128)(2,1)S(1)}, u32[]{:S(2)}, u32[]{:S(2)}) async-start(bf16[64,3,3072]{2,1,0:T(4,128)(2,1)} %bitcast.7), calls=%async_computation | async-start | bytes 3145728 | tf_op jit(solution)/shard_map/all_to_all | solution.py:41
  28.5 18.3 %all-to-all-done = bf16[64,3,3072]{2,1,0:T(4,128)(2,1)S(1)} async-done(((bf16[64,3,3072]{2,1,0:T(4,128)(2,1)}), bf16[64,3,3072]{2,1,0:T(4,128)(2,1)S(1)}, u32[]{:S(2)}, u32[]{:S(2)}) %all-to-all-start) | async-done | bytes 1179680 | tf_op jit(solution)/shard_map/all_to_all | solution.py:41
  61.3 5.0 all-to-all-start.1
  71.3 18.4 %all-to-all-done.1 = bf16[64,3,3072]{2,1,0:T(4,128)(2,1)S(1)} async-done(((bf16[64,3,3072]{2,1,0:T(4,128)(2,1)}), bf16[64,3,3072]{2,1,0:T(4,128)(2,1)S(1)}, u32[]{:S(2)}, u32[]{:S(2)}) %all-to-all-start.1) | async-done | bytes 1179680 | tf_op jit(solution)/shard_map/all_to_all | solution.py:48
  92.6 5.4 collective-permute-start
  104.1 5.7 all-to-all-start.2
  112.8 20.4 %all-to-all-done.2 = bf16[64,3,3072]{2,1,0:T(4,128)(2,1)} async-done(((bf16[64,3,3072]{2,1,0:T(4,128)(2,1)}), bf16[64,3,3072]{2,1,0:T(4,128)(2,1)}, u32[]{:S(2)}, u32[]{:S(2)}) %all-to-all-start.2) | async-done | bytes 1179680 | tf_op jit(solution)/shard_map/all_to_all | solution.py:41
  136.1 5.4 bitcast_dynamic-update-slice_fusion.4
  147.7 5.1 all-to-all-start.3
  155.3 20.9 %all-to-all-done.3 = bf16[64,3,3072]{2,1,0:T(4,128)(2,1)S(1)} async-done(((bf16[64,3,3072]{2,1,0:T(4,128)(2,1)}), bf16[64,3,3072]{2,1,0:T(4,128)(2,1)S(1)}, u32[]{:S(2)}, u32[]{:S(2)}) %all-to-all-start.3) | async-done | bytes 1179680 | tf_op jit(solution)/shard_map/all_to_all | solution.py:48
  180.0 5.1 collective-permute-start.1
  189.3 6.1 %all-to-all-start.4 = ((bf16[64,3,3072]{2,1,0:T(4,128)(2,1)}), bf16[64,3,3072]{2,1,0:T(4,128)(2,1)}, u32[]{:S(2)}, u32[]{:S(2)}) async-start(bf16[64,3,3072]{2,1,0:T(4,128)(2,1)} %bitcast.26), calls=%async_computation.4 | async-start | bytes 3145728 | tf_op jit(solution)/shard_map/all_to_all | solution.py:41
  197.7 20.9 %all-to-all-done.4 = bf16[64,3,3072]{2,1,0:T(4,128)(2,1)} async-done(((bf16[64,3,3072]{2,1,0:T(4,128)(2,1)}), bf16[64,3,3072]{2,1,0:T(4,128)(2,1)}, u32[]{:S(2)}, u32[]{:S(2)}) %all-to-all-start.4) | async-done | bytes 1179680 | tf_op jit(solution)/shard_map/all_to_all | solution.py:41
  221.6 5.4 bitcast_dynamic-update-slice_fusion.3
  233.2 4.9 all-to-all-start.5
  240.4 21.2 %all-to-all-done.5 = bf16[64,3,3072]{2,1,0:T(4,128)(2,1)S(1)} async-done(((bf16[64,3,3072]{2,1,0:T(4,128)(2,1)}), bf16[64,3,3072]{2,1,0:T(4,128)(2,1)S(1)}, u32[]{:S(2)}, u32[]{:S(2)}) %all-to-all-start.5) | async-done | bytes 1179680 | tf_op jit(solution)/shard_map/all_to_all | solution.py:48
  266.8 5.8 %all-to-all-start.6 = ((bf16[64,3,3072]{2,1,0:T(4,128)(2,1)}), bf16[64,3,3072]{2,1,0:T(4,128)(2,1)}, u32[]{:S(2)}, u32[]{:S(2)}) async-start(bf16[64,3,3072]{2,1,0:T(4,128)(2,1)} %bitcast.568), calls=%async_computation.6 | async-start | bytes 3145728 | tf_op jit(solution)/shard_map/all_to_all | solution.py:41
  274.8 21.1 %all-to-all-done.6 = bf16[64,3,3072]{2,1,0:T(4,128)(2,1)} async-done(((bf16[64,3,3072]{2,1,0:T(4,128)(2,1)}), bf16[64,3,3072]{2,1,0:T(4,128)(2,1)}, u32[]{:S(2)}, u32[]{:S(2)}) %all-to-all-start.6) | async-done | bytes 1179680 | tf_op jit(solution)/shard_map/all_to_all | solution.py:41
  298.8 5.2 fusion.4
  312.1 5.0 all-to-all-start.7
  317.9 22.5 %all-to-all-done.7 = bf16[64,3,3072]{2,1,0:T(4,128)(2,1)S(1)} async-done(((bf16[64,3,3072]{2,1,0:T(4,128)(2,1)}), bf16[64,3,3072]{2,1,0:T(4,128)(2,1)S(1)}, u32[]{:S(2)}, u32[]{:S(2)}) %all-to-all-start.7) | async-done | bytes 1179680 | tf_op jit(solution)/shard_map/all_to_all | solution.py:48
  344.3 5.2 collective-permute-done.2
  352.4 5.9 %all-to-all-start.8 = ((bf16[64,3,3072]{2,1,0:T(4,128)(2,1)}), bf16[64,3,3072]{2,1,0:T(4,128)(2,1)}, u32[]{:S(2)}, u32[]{:S(2)}) async-start(bf16[64,3,3072]{2,1,0:T(4,128)(2,1)} %bitcast.68), calls=%async_computation.8 | async-start | bytes 3145728 | tf_op jit(solution)/shard_map/all_to_all | solution.py:41
  358.9 22.6 %all-to-all-done.8 = bf16[64,3,3072]{2,1,0:T(4,128)(2,1)} async-done(((bf16[64,3,3072]{2,1,0:T(4,128)(2,1)}), bf16[64,3,3072]{2,1,0:T(4,128)(2,1)}, u32[]{:S(2)}, u32[]{:S(2)}) %all-to-all-start.8) | async-done | bytes 1179680 | tf_op jit(solution)/shard_map/all_to_all | solution.py:41
  385.5 5.5 fusion.2
  405.3 22.2 %all-to-all-done.9 = bf16[64,3,3072]{2,1,0:T(4,128)(2,1)S(1)} async-done(((bf16[64,3,3072]{2,1,0:T(4,128)(2,1)}), bf16[64,3,3072]{2,1,0:T(4,128)(2,1)S(1)}, u32[]{:S(2)}, u32[]{:S(2)}) %all-to-all-start.9) | async-done | bytes 1179680 | tf_op jit(solution)/shard_map/all_to_all | solution.py:48
  430.6 5.9 %collective-permute-done.3 = bf16[8,3072]{1,0:T(8,128)(2,1)S(1)} collective-permute-done((bf16[8,3072]{1,0:T(8,128)(2,1)S(1)}, bf16[8,3072]{1,0:T(8,128)(2,1)S(1)}, u32[]{:S(2)}, u32[]{:S(2)}) %collective-permute-start.3) | collective-permute-done | bytes 49184 | tf_op jit(solution)/shard_map/ppermute | solution.py:12
  439.8 32.3 %all_to_all.60 = bf16[64,3,3072]{2,1,0:T(4,128)(2,1)} all-to-all(bf16[64,3,3072]{2,1,0:T(4,128)(2,1)S(1)} %bitcast.569), channel_id=1, replica_groups=mesh['section'=2,'expert'=8,'dp'=8] {'expert','dp'}, dimensions={0} | all-to-all | bytes 2359296 | tf_op jit(solution)/shard_map/all_to_all | solution.py:41
  476.1 5.5 fusion
  489.8 5.4 all-to-all-start.11
  495.5 26.4 %all-to-all-done.11 = bf16[64,3,3072]{2,1,0:T(4,128)(2,1)S(1)} async-done(((bf16[64,3,3072]{2,1,0:T(4,128)(2,1)}), bf16[64,3,3072]{2,1,0:T(4,128)(2,1)S(1)}, u32[]{:S(2)}, u32[]{:S(2)}) %all-to-all-start.11) | async-done | bytes 1179680 | tf_op jit(solution)/shard_map/all_to_all | solution.py:48
  523.5 42.6 %all-gather.3.cloned.1.call-done = f32[196608,8]{0,1:T(8,128)} async-done(((f32[3072,8]{0,1:T(8,128)}), f32[196608,8]{0,1:T(8,128)}) %all-gather.3.cloned.1.call-update) | async-done | bytes 6291472 | tf_op jit(solution)/shard_map/all_gather | solution.py:222
  (469 shorter events, 143.9 us)
Async XLA Ops:
  13.8 33.0 %all-to-all-start = ((bf16[64,3,3072]{2,1,0:T(4,128)(2,1)}), bf16[64,3,3072]{2,1,0:T(4,128)(2,1)S(1)}, u32[]{:S(2)}, u32[]{:S(2)}) async-start(bf16[64,3,3072]{2,1,0:T(4,128)(2,1)} %bitcast.7), calls=%async_computation | async-start | bytes 3145728 | tf_op jit(solution)/shard_map/all_to_all | solution.py:41
  28.5 38.4 %copy-start.24 = (f32[8,3072]{1,0:T(8,128)}, f32[8,3072]{1,0:T(8,128)S(1)}, u32[]{:S(2)}) copy-start(f32[8,3072]{1,0:T(8,128)S(1)} %bitcast_convert_fusion) | copy-start | bytes 294916
  57.0 41.0 %copy-start.1 = (f32[2,192,1024]{2,1,0:T(8,128)}, f32[2,192,1024]{2,1,0:T(8,128)S(1)}, u32[]{:S(2)}) copy-start(f32[2,192,1024]{2,1,0:T(8,128)S(1)} %get-tuple-element.57) | copy-start | bytes 4718596
  61.3 28.4 %all-to-all-start.1 = ((bf16[64,3,3072]{2,1,0:T(4,128)(2,1)}), bf16[64,3,3072]{2,1,0:T(4,128)(2,1)S(1)}, u32[]{:S(2)}, u32[]{:S(2)}) async-start(bf16[64,3,3072]{2,1,0:T(4,128)(2,1)} %reshape.574), calls=%async_computation.1 | async-start | bytes 3145728 | tf_op jit(solution)/shard_map/all_to_all | solution.py:48
  92.6 7.9 %collective-permute-start = (bf16[8,3072]{1,0:T(8,128)(2,1)S(1)}, bf16[8,3072]{1,0:T(8,128)(2,1)S(1)}, u32[]{:S(2)}, u32[]{:S(2)}) collective-permute-start(bf16[8,3072]{1,0:T(8,128)(2,1)S(1)} %fusion.158), channel_id=1, source_target_pairs={{0,64},{1,65},{2,66},{3,67},{4,68},{5,69},{6,70},{7,71},{8,72},{9,... | collective-permute-start | bytes 147464 | tf_op jit(solution)/shard_map/ppermute | solution.py:12
  104.1 29.1 %all-to-all-start.2 = ((bf16[64,3,3072]{2,1,0:T(4,128)(2,1)}), bf16[64,3,3072]{2,1,0:T(4,128)(2,1)}, u32[]{:S(2)}, u32[]{:S(2)}) async-start(bf16[64,3,3072]{2,1,0:T(4,128)(2,1)} %bitcast.17), calls=%async_computation.2 | async-start | bytes 3145728 | tf_op jit(solution)/shard_map/all_to_all | solution.py:41
  147.7 28.5 %all-to-all-start.3 = ((bf16[64,3,3072]{2,1,0:T(4,128)(2,1)}), bf16[64,3,3072]{2,1,0:T(4,128)(2,1)S(1)}, u32[]{:S(2)}, u32[]{:S(2)}) async-start(bf16[64,3,3072]{2,1,0:T(4,128)(2,1)} %reshape.580), calls=%async_computation.3 | async-start | bytes 3145728 | tf_op jit(solution)/shard_map/all_to_all | solution.py:48
  155.3 23.5 %copy-start.53 = (s32[8,2]{0,1:T(2,128)S(1)}, s32[8,2]{0,1:T(2,128)}, u32[]{:S(2)}) copy-start(s32[8,2]{0,1:T(2,128)} %multiply_add_fusion.4) | copy-start | bytes 196
  155.3 29.8 %copy-start.4 = (f32[2,192,1024]{2,1,0:T(8,128)S(1)}, f32[2,192,1024]{2,1,0:T(8,128)}, u32[]{:S(2)}) copy-start(f32[2,192,1024]{2,1,0:T(8,128)} %copy-done.3) | copy-start | bytes 4718596
  180.0 17.6 %copy-start.28 = (bf16[2,8,3072]{2,1,0:T(8,128)(2,1)}, bf16[2,8,3072]{2,1,0:T(8,128)(2,1)S(1)}, u32[]{:S(2)}) copy-start(bf16[2,8,3072]{2,1,0:T(8,128)(2,1)S(1)} %get-tuple-element.27) | copy-start | bytes 294916
  180.0 6.8 %collective-permute-start.1 = (bf16[8,3072]{1,0:T(8,128)(2,1)S(1)}, bf16[8,3072]{1,0:T(8,128)(2,1)S(1)}, u32[]{:S(2)}, u32[]{:S(2)}) collective-permute-start(bf16[8,3072]{1,0:T(8,128)(2,1)S(1)} %get-tuple-element.28), channel_id=1, source_target_pairs={{0,64},{1,65},{2,66},{3,67},{4,68},{5,69},{6,70},{7,71},{8,72},{9,... | collective-permute-start | bytes 147464 | tf_op jit(solution)/shard_map/ppermute | solution.py:12
  189.3 29.4 %all-to-all-start.4 = ((bf16[64,3,3072]{2,1,0:T(4,128)(2,1)}), bf16[64,3,3072]{2,1,0:T(4,128)(2,1)}, u32[]{:S(2)}, u32[]{:S(2)}) async-start(bf16[64,3,3072]{2,1,0:T(4,128)(2,1)} %bitcast.26), calls=%async_computation.4 | async-start | bytes 3145728 | tf_op jit(solution)/shard_map/all_to_all | solution.py:41
  233.2 28.4 %all-to-all-start.5 = ((bf16[64,3,3072]{2,1,0:T(4,128)(2,1)}), bf16[64,3,3072]{2,1,0:T(4,128)(2,1)S(1)}, u32[]{:S(2)}, u32[]{:S(2)}) async-start(bf16[64,3,3072]{2,1,0:T(4,128)(2,1)} %reshape.586), calls=%async_computation.5 | async-start | bytes 3145728 | tf_op jit(solution)/shard_map/all_to_all | solution.py:48
  240.3 22.2 %copy-start.52 = (s32[8,2]{0,1:T(2,128)S(1)}, s32[8,2]{0,1:T(2,128)}, u32[]{:S(2)}) copy-start(s32[8,2]{0,1:T(2,128)} %multiply_add_fusion.3) | copy-start | bytes 196
  240.4 22.4 %copy-start.18 = (f32[2,8,2,3072]{3,1,2,0:T(8,128)S(1)}, f32[2,8,2,3072]{3,1,2,0:T(8,128)}, u32[]{:S(2)}) copy-start(f32[2,8,2,3072]{3,1,2,0:T(8,128)} %copy-done.17) | copy-start | bytes 1179652
  240.4 22.4 %copy-start.35 = (f32[1,8,2,3072]{3,1,2,0:T(8,128)S(1)}, f32[1,8,2,3072]{3,1,2,0:T(8,128)}, u32[]{:S(2)}) copy-start(f32[1,8,2,3072]{3,1,2,0:T(8,128)} %constant_dynamic-slice_fusion.6) | copy-start | bytes 589828
  266.8 37.1 %slice-start = ((s8[6291456]{0:T(1024)(128)(4,1)}), s8[2097152]{0:T(1024)(128)(4,1)S(1)}, s32[]{:S(2)}) async-start(s8[6291456]{0:T(1024)(128)(4,1)} %bitcast.549), calls=%async_computation.13 | async-start | bytes 4194304
  266.8 29.2 %all-to-all-start.6 = ((bf16[64,3,3072]{2,1,0:T(4,128)(2,1)}), bf16[64,3,3072]{2,1,0:T(4,128)(2,1)}, u32[]{:S(2)}, u32[]{:S(2)}) async-start(bf16[64,3,3072]{2,1,0:T(4,128)(2,1)} %bitcast.568), calls=%async_computation.6 | async-start | bytes 3145728 | tf_op jit(solution)/shard_map/all_to_all | solution.py:41
  312.1 28.4 %all-to-all-start.7 = ((bf16[64,3,3072]{2,1,0:T(4,128)(2,1)}), bf16[64,3,3072]{2,1,0:T(4,128)(2,1)S(1)}, u32[]{:S(2)}, u32[]{:S(2)}) async-start(bf16[64,3,3072]{2,1,0:T(4,128)(2,1)} %reshape.592), calls=%async_computation.7 | async-start | bytes 3145728 | tf_op jit(solution)/shard_map/all_to_all | solution.py:48
  317.9 24.0 %copy-start.39 = (bf16[2,8,3072]{2,1,0:T(8,128)(2,1)S(1)}, bf16[2,8,3072]{2,1,0:T(8,128)(2,1)}, u32[]{:S(2)}) copy-start(bf16[2,8,3072]{2,1,0:T(8,128)(2,1)} %param.11) | copy-start | bytes 294916
  317.9 24.0 %copy-start.57 = (f32[8]{0:T(128)S(1)}, f32[8]{0:T(128)}, u32[]{:S(2)}) copy-start(f32[8]{0:T(128)} %copy-done.56) | copy-start | bytes 100
  317.9 24.0 %copy-start.63 = (f32[8]{0:T(128)S(1)}, f32[8]{0:T(128)}, u32[]{:S(2)}) copy-start(f32[8]{0:T(128)} %get-tuple-element.49) | copy-start | bytes 100
  342.1 7.5 %collective-permute-start.2 = (bf16[8,3072]{1,0:T(8,128)(2,1)S(1)}, bf16[8,3072]{1,0:T(8,128)(2,1)S(1)}, u32[]{:S(2)}, u32[]{:S(2)}) collective-permute-start(bf16[8,3072]{1,0:T(8,128)(2,1)S(1)} %get-tuple-element.18), channel_id=1, source_target_pairs={{64,0},{65,1},{66,2},{67,3},{68,4},{69,5},{70,6},{71,7},{72,8},{73... | collective-permute-start | bytes 147464 | tf_op jit(solution)/shard_map/ppermute | solution.py:12
  352.4 29.2 %all-to-all-start.8 = ((bf16[64,3,3072]{2,1,0:T(4,128)(2,1)}), bf16[64,3,3072]{2,1,0:T(4,128)(2,1)}, u32[]{:S(2)}, u32[]{:S(2)}) async-start(bf16[64,3,3072]{2,1,0:T(4,128)(2,1)} %bitcast.68), calls=%async_computation.8 | async-start | bytes 3145728 | tf_op jit(solution)/shard_map/all_to_all | solution.py:41
  358.6 32.3 %slice-start.2 = ((s8[6291456]{0:T(1024)(128)(4,1)}), s8[2097152]{0:T(1024)(128)(4,1)S(1)}, s32[]{:S(2)}) async-start(s8[6291456]{0:T(1024)(128)(4,1)} %bitcast.551), calls=%async_computation.15 | async-start | bytes 4194304
  399.1 28.4 %all-to-all-start.9 = ((bf16[64,3,3072]{2,1,0:T(4,128)(2,1)}), bf16[64,3,3072]{2,1,0:T(4,128)(2,1)S(1)}, u32[]{:S(2)}, u32[]{:S(2)}) async-start(bf16[64,3,3072]{2,1,0:T(4,128)(2,1)} %reshape.598), calls=%async_computation.9 | async-start | bytes 3145728 | tf_op jit(solution)/shard_map/all_to_all | solution.py:48
  404.0 162.1 %all-gather.3.cloned.1.call-start = ((), (), s32[]{:S(2)}) async-start(), calls=%async_computation.12 | async-start | bytes 6389760 | tf_op jit(solution)/shard_map/all_gather | solution.py:222
  429.0 7.5 %collective-permute-start.3 = (bf16[8,3072]{1,0:T(8,128)(2,1)S(1)}, bf16[8,3072]{1,0:T(8,128)(2,1)S(1)}, u32[]{:S(2)}, u32[]{:S(2)}) collective-permute-start(bf16[8,3072]{1,0:T(8,128)(2,1)S(1)} %get-tuple-element.12), channel_id=1, source_target_pairs={{64,0},{65,1},{66,2},{67,3},{68,4},{69,5},{70,6},{71,7},{72,8},{73... | collective-permute-start | bytes 147464 | tf_op jit(solution)/shard_map/ppermute | solution.py:12
  439.8 41.8 %slice-start.4 = ((s8[6291456]{0:T(1024)(128)(4,1)}), s8[2097152]{0:T(1024)(128)(4,1)S(1)}, s32[]{:S(2)}) async-start(s8[6291456]{0:T(1024)(128)(4,1)} %bitcast.553), calls=%async_computation.17 | async-start | bytes 4194304
  489.8 32.2 %all-to-all-start.11 = ((bf16[64,3,3072]{2,1,0:T(4,128)(2,1)}), bf16[64,3,3072]{2,1,0:T(4,128)(2,1)S(1)}, u32[]{:S(2)}, u32[]{:S(2)}) async-start(bf16[64,3,3072]{2,1,0:T(4,128)(2,1)} %reshape.604), calls=%async_computation.11 | async-start | bytes 3145728 | tf_op jit(solution)/shard_map/all_to_all | solution.py:48
  495.4 27.6 %copy-start.43 = (bf16[1,2,8,3072]{3,2,1,0:T(8,128)(2,1)}, bf16[1,2,8,3072]{3,2,1,0:T(8,128)(2,1)S(1)}, u32[]{:S(2)}) copy-start(bf16[1,2,8,3072]{3,2,1,0:T(8,128)(2,1)S(1)} %fusion.175) | copy-start | bytes 294916
  523.5 46.4 %copy-start.42 = (bf16[1,2,8,3072]{3,2,1,0:T(8,128)(2,1)}, bf16[1,2,8,3072]{3,2,1,0:T(8,128)(2,1)S(1)}, u32[]{:S(2)}) copy-start(bf16[1,2,8,3072]{3,2,1,0:T(8,128)(2,1)S(1)} %fusion.187) | copy-start | bytes 294916
  (72 other events, 361.2 us)
Sparse Core Ops, SparseCore 0:
  438.2 127.9 all-gather.2
